TPU v7x, 32 devices: a whole 2x2x4 slice. The times are simulated.
32 devices in a mesh: grp: 2 (over x), patch: 16 (over z, y, core).
Axes of the slice: x: 2, y: 2, z: 4, core: 2. Of those that a mesh axis runs over, the one named last changes fastest.
Arguments:
- displace: float32 [2, 32768, 384], P('grp', 'patch'), may hold values from -6 to 6
- velocity: float32 [2, 32768, 384], P('grp', 'patch'), may hold values from -6 to 6
- ext_force: float32 [2, 32768, 384], P('grp', 'patch'), may hold values from -6 to 6
- inv_mass: float32 [2, 32768, 128], P('grp', 'patch'), may hold values from 0.1 to 6
- thickness: float32 [2, 32768, 128], P('grp', 'patch'), may hold values from 0.5 to 2
- stiff_bands: bfloat16 [5, 384, 384], replicated, may hold values from -0.125 to 0.125
- pair_points: int32 [2, 16, 3, 1536], P('grp', 'patch'), may hold values from 0 to 6143
- pair_weights: float32 [2, 16, 3, 1536], P('grp', 'patch'), may hold values from 0.25 to 1
Outputs:
- displace_new: float32 [2, 32768, 384], P('grp', 'patch')
- velocity_new: float32 [2, 32768, 384], P('grp', 'patch')
Inputs may be any that keep to these rules, and one draw needn't show every extreme that they name: `pair_points`: entry e names the control point in row e // 3 of the sending block (rows counted within the block) and point e % 3 across the strip.
All inputs are finite; a program needn't handle non-finite values.
Results may differ from a plain program's by a relative error of at most 0.00094.
The roundings to bfloat16 on the way count: a program that leaves them out, or rounds other values in their place, can miss the bound.
Values may be sent and summed in bfloat16 or wider, within the bound.
A program may use at most 192 MiB of HBM per device.

v0:
```python
import jax
import jax.numpy as jnp
from jax import lax
from jax.sharding import PartitionSpec as P

POINTS = 128
REACH = 2
SUBSTEPS = 4
EDGE = 3


PENALTY = 1.0
DAMPING = 0.5
COURANT = 0.4


def partner_2(block, axis, apart):
    count = lax.axis_size(axis)
    route = []
    for low in range(count):
        high = low | 1 << apart
        if high != low and high < count:
            route += [(low, high), (high, low)]
    return lax.ppermute(block, axis, route)


def passed_along(block, axis, distance):
    devices = range(lax.axis_size(axis))
    route = [(i - distance, i) for i in devices if i - distance in devices]
    return lax.ppermute(block, axis, route)


def padded_2(cells, sides, width):
    for axis, dim in sides:
        count = lax.axis_size(axis)
        ends = count - 1
        head = lax.slice_in_dim(cells, 0, width, axis=dim)
        tail = lax.slice_in_dim(cells, cells.shape[dim] - width, cells.shape[dim], axis=dim)
        cells = jnp.concatenate(
            [
                lax.ppermute(tail, axis, [(i, (i + 1) % count) for i in range(ends)]),
                cells,
                lax.ppermute(head, axis, [((i + 1) % count, i) for i in range(ends)]),
            ],
            axis=dim,
        )
    return cells


def band_force(padded, thickness, stiff_bands):
    row_count = padded.shape[0] - 2 * REACH
    summed = jnp.zeros((row_count, stiff_bands.shape[2]), jnp.float32)
    for band_index in range(2 * REACH + 1):
        summed = summed + jnp.dot(
            padded[band_index : band_index + row_count],
            stiff_bands[band_index],
            preferred_element_type=jnp.float32,
        )
    return (summed.reshape(row_count, 3, POINTS) * thickness[:, None, :]).reshape(
        row_count, 3 * POINTS
    )


def advance(field, moving, ext_force, coupling, inner_force, inv_mass, step_size):
    row_count = field.shape[0]
    accel_now = (
        (ext_force + coupling - inner_force).reshape(row_count, 3, POINTS) * inv_mass[:, None, :]
    ).reshape(row_count, 3 * POINTS)
    moved_vel = moving + step_size * accel_now
    return (field + step_size * moved_vel, moved_vel)


def edge_values(values):
    row_count = values.shape[0]
    return (
        values.reshape(row_count, 3, POINTS)[:, :, :EDGE]
        .transpose(1, 0, 2)
        .reshape(3, row_count * EDGE)
    )


def interface_force(field, moving, inner_force, pair_table, pair_weight):
    row_count = field.shape[0]
    row_width = field.shape[1]
    point_total = row_count * EDGE
    slot_count = pair_table.shape[1]
    block_size = 512
    block_total = slot_count // block_size
    table_blocks = pair_table.reshape(3, block_total, block_size).transpose(1, 0, 2)
    candidates = jnp.arange(point_total, dtype=jnp.int32)
    edge_matrix = jnp.concatenate(
        [edge_values(field), edge_values(moving), edge_values(inner_force)], axis=0
    )

    def selector(table_block):
        return (table_block[:, :, None] == candidates[None, None, :]).astype(jnp.float32)

    def pick_block(table_block):
        return jnp.einsum(
            "qp,jbp->qjb", edge_matrix, selector(table_block), precision=lax.Precision.HIGHEST
        )

    picked = lax.map(pick_block, table_blocks)
    outgoing = picked.transpose(1, 2, 0, 3).reshape(9, 3, slot_count)
    gathered = outgoing.reshape(3, 3, 3, slot_count)
    swapped = partner_2(outgoing.astype(jnp.bfloat16), "grp", 0).astype(outgoing.dtype)
    from_below = passed_along(swapped[:, 2].astype(jnp.bfloat16), "patch", 1).astype(jnp.float32)
    from_above = passed_along(swapped[:, 0].astype(jnp.bfloat16), "patch", -1).astype(jnp.float32)
    arrived = jnp.stack([from_below, swapped[:, 1], from_above], axis=1)
    partner = arrived.reshape(3, 3, 3, slot_count)
    block_index = lax.axis_index("patch")
    neighbour = block_index + jnp.arange(3, dtype=jnp.int32) - 1
    present = ((neighbour >= 0) & (neighbour < lax.axis_size("patch"))).astype(jnp.float32)
    weight = pair_weight * present[:, None]
    slot_force = weight[None] * (
        -PENALTY * (gathered[0] - partner[0])
        - DAMPING * (gathered[1] - partner[1])
        + 0.5 * (partner[2] - gathered[2])
    )
    force_blocks = slot_force.reshape(3, 3, block_total, block_size).transpose(2, 0, 1, 3)

    def spread_block(total, pieces):
        table_block, force_block = pieces
        return (
            total
            + jnp.einsum(
                "cjb,jbp->cp", force_block, selector(table_block), precision=lax.Precision.HIGHEST
            ),
            None,
        )

    edge_coupling, unused = lax.scan(
        spread_block, jnp.zeros((3, point_total), jnp.float32), (table_blocks, force_blocks)
    )
    placed = edge_coupling.reshape(3, row_count, EDGE).transpose(1, 0, 2)
    coupling = jnp.pad(placed, ((0, 0), (0, 0), (0, POINTS - EDGE)))
    return coupling.reshape(row_count, row_width)


def per_device(
    displace, velocity, ext_force, inv_mass, thickness, stiff_bands, pair_points, pair_weights
):
    field = displace[0]
    moving = velocity[0]
    outer_force = ext_force[0]
    mass_inverse = inv_mass[0]
    thick_local = thickness[0]
    pair_table = pair_points[0, 0]
    pair_weight = pair_weights[0, 0]
    tile_count = field.shape[0]
    row_width = field.shape[1]
    point_count = mass_inverse.shape[1]
    group_index = lax.axis_index("grp")
    local_limit = jnp.min(1.0 / jnp.sqrt(mass_inverse * thick_local))
    base_step = COURANT * lax.pmin(local_limit, ("grp", "patch"))
    step_size = jnp.where(group_index == 0, SUBSTEPS * base_step, base_step)
    depth_rows = REACH * SUBSTEPS
    bundle = jnp.concatenate([field, moving, outer_force, mass_inverse, thick_local], axis=1)
    extended = padded_2(bundle, (("patch", 0),), depth_rows)
    wide_field = extended[:, :row_width]
    wide_moving = extended[:, row_width : 2 * row_width]
    wide_outer = extended[:, 2 * row_width : 3 * row_width]
    wide_mass = extended[:, 3 * row_width : 3 * row_width + point_count]
    wide_thick = extended[:, 3 * row_width + point_count :]

    def wide_force(current):
        padded = jnp.pad(current.astype(jnp.bfloat16), ((REACH, REACH), (0, 0)))
        return band_force(padded, wide_thick, stiff_bands)

    first_force = wide_force(wide_field)
    center_force = first_force[depth_rows : depth_rows + tile_count]
    coupling = interface_force(field, moving, center_force, pair_table, pair_weight)
    wide_coupling = padded_2(coupling, (("patch", 0),), depth_rows)
    for substep in range(SUBSTEPS):
        inner_force = first_force if substep == 0 else wide_force(wide_field)
        new_field, new_moving = advance(
            wide_field, wide_moving, wide_outer, wide_coupling, inner_force, wide_mass, step_size
        )
        if substep == 0:
            wide_field, wide_moving = (new_field, new_moving)
        else:
            wide_field = jnp.where(group_index == 1, new_field, wide_field)
            wide_moving = jnp.where(group_index == 1, new_moving, wide_moving)
    center_field = wide_field[depth_rows : depth_rows + tile_count]
    center_moving = wide_moving[depth_rows : depth_rows + tile_count]
    return (center_field[None], center_moving[None])


def solution(mesh):
    return jax.shard_map(
        per_device,
        mesh=mesh,
        in_specs=(
            P("grp", "patch", None),
            P("grp", "patch", None),
            P("grp", "patch", None),
            P("grp", "patch", None),
            P("grp", "patch", None),
            P(),
            P("grp", "patch", None, None),
            P("grp", "patch", None, None),
        ),
        out_specs=(P("grp", "patch", None), P("grp", "patch", None)),
        check_vma=False,
    )
```

profile of v0, /device:TPU:0, one launch (start us, length us, event | category | flops | bytes accessed | tf_op | source)
XLA Modules:
  0.0 318.7 jit_solution(7432654980971494082)
XLA Ops:
  0.6 4.0 %bitcast_dynamic-update-slice_fusion.2 = f32[2048,1408]{1,0:T(8,128)} fusion(f32[1,2048,384]{2,1,0:T(8,128)} %param.12), kind=kLoop, calls=%fused_computation.59 | loop fusion | bytes 6291456
  4.7 1.9 bitcast_dynamic-update-slice_fusion.1
  7.7 2.0 bitcast_dynamic-update-slice_fusion
  10.8 2.0 bitcast_dynamic-update-slice_fusion.3
  12.7 1.4 fusion.138
  14.2 2.4 collective-permute-start
  16.6 1.3 collective-permute-start.1
  17.9 2.4 copy.64
  20.3 2.4 copy.66
  24.9 2.4 reshape.107
  28.4 2.4 reshape.108
  30.8 5.5 %pad_maximum_fusion = f32[2064,1408]{1,0:T(8,128)S(1)} fusion(f32[8,1408]{1,0:T(8,128)S(1)} %collective-permute-done.1, f32[2048,1408]{1,0:T(8,128)} %get-tuple-element.141, f32[8,1408]{1,0:T(8,128)S(1)} %collective-permute-done), kind=kLoop, calls=%fused_computation.16 | loop fusion | flops 5812224 | bytes 23248896 | tf_op jit(solution)/shard_map/concatenate | solution.py:39
  36.5 2.3 copy-done.10
  38.8 3.0 fusion.46
  41.8 3.0 fusion.49
  44.8 3.0 pad_maximum_fusion.2
  47.8 2.6 copy.69
  51.4 3.3 %convolution_add_fusion.14 = f32[2064,384]{1,0:T(8,128)S(1)} fusion(f32[2064,384]{1,0:T(8,128)} %fusion.49, bf16[2064,384]{1,0:T(8,128)(2,1)S(1)} %slice.392, bf16[5,384,384]{2,1,0:T(8,128)(2,1)S(1)} %copy-done.10), kind=kOutput, calls=%fused_computation.47 | convolution fusion | flops 609490944 | bytes 8220672 | tf_op jit(solution)/shard_map/dot_general | solution.py:54
  54.7 3.3 %fusion.24 = f32[2064,384]{1,0:T(8,128)S(1)} fusion(f32[2064,384]{1,0:T(8,128)S(1)} %copy-done.9, f32[2064,384]{1,0:T(8,128)S(1)} %convolution_add_fusion.14, bf16[5,384,384]{2,1,0:T(8,128)(2,1)S(1)} %copy-done.10, f32[2064,1408]{1,0:T(8,128)} %copy-done), kind=kOutput, calls=%fused_computation.46 | convolution fusion | flops 610283520 | bytes 11390976 | tf_op jit(solution)/shard_map/dot_general | solution.py:54
  58.0 3.0 convolution_add_fusion.12
  60.9 3.2 %copy.68 = f32[2064,384]{0,1:T(8,128)S(1)} copy(f32[2064,384]{1,0:T(8,128)} %convolution_add_fusion.12) | data formatting | bytes 6340608 | tf_op jit(solution)/shard_map/add | solution.py:54
  65.4 2.4 reshape.110
  68.8 55.8 %while.22 = (s32[]{:T(128)}, f32[3,9,3,512]{3,0,2,1:T(4,128)S(1)}, s32[3,3,512]{2,1,0:T(4,128)S(1)}, f32[9,6144]{1,0:T(8,128)S(1)}, s32[]{:T(128)}, /*index=5*/s32[]{:T(128)}) while((s32[]{:T(128)}, f32[3,9,3,512]{3,0,2,1:T(4,128)S(1)}, s32[3,3,512]{2,1,0:T(4,128)S(1)}, f32[9,6144]{1,0:T(8,128)S(1)}, s32[]{:T(128)}, ...), condition=%wide.region_3.4_spmd.clone, body=%wide.region_2.3_spmd.clone.sunk | while | flops 1028653056 | bytes 516181 | solution.py:103
  69.1 16.9 %fusion.147 = f32[1,9,3,512]{3,1,2,0:T(8,128)S(1)} fusion(s32[3,512]{1,0:T(4,128)S(1)} %dynamic-slice_bitcast_fusion.4, f32[9,6144]{1,0:T(8,128)S(1)} %get-tuple-element.216), kind=kOutput, calls=%fused_computation.5.clone.1 | convolution fusion | flops 1028653056 | bytes 282624 | tf_op jit(solution)/shard_map/while/body/eval_jaxpr/qp,jbp->qjb/dot_general | solution.py:99
  86.0 1.4 dynamic_update_slice.6
  87.4 16.9 %fusion.147 = f32[1,9,3,512]{3,1,2,0:T(8,128)S(1)} fusion(s32[3,512]{1,0:T(4,128)S(1)} %dynamic-slice_bitcast_fusion.4, f32[9,6144]{1,0:T(8,128)S(1)} %get-tuple-element.216), kind=kOutput, calls=%fused_computation.5.clone.1 | convolution fusion | flops 1028653056 | bytes 282624 | tf_op jit(solution)/shard_map/while/body/eval_jaxpr/qp,jbp->qjb/dot_general | solution.py:99
  104.4 1.4 dynamic_update_slice.6
  105.8 16.9 %fusion.147 = f32[1,9,3,512]{3,1,2,0:T(8,128)S(1)} fusion(s32[3,512]{1,0:T(4,128)S(1)} %dynamic-slice_bitcast_fusion.4, f32[9,6144]{1,0:T(8,128)S(1)} %get-tuple-element.216), kind=kOutput, calls=%fused_computation.5.clone.1 | convolution fusion | flops 1028653056 | bytes 282624 | tf_op jit(solution)/shard_map/while/body/eval_jaxpr/qp,jbp->qjb/dot_general | solution.py:99
  122.7 1.4 dynamic_update_slice.6
  124.8 2.4 collective-permute-start.2
  127.1 2.7 collective-permute-done.2
  130.0 1.3 collective-permute-start.4
  131.3 4.3 %collective-permute-start.3 = (bf16[9,1536]{1,0:T(8,128)(2,1)S(1)}, bf16[9,1536]{1,0:T(8,128)(2,1)S(1)}, u32[]{:S(2)}, u32[]{:S(2)}) collective-permute-start(bf16[9,1536]{1,0:T(8,128)(2,1)S(1)} %bitcast.142), channel_id=1, source_target_pairs={{0,1},{1,2},{2,3},{3,4},{4,5},{5,6},{6,7},{7,8},{8,9},{9,10},{10,1... | collective-permute-start | bytes 82952 | tf_op jit(solution)/shard_map/ppermute | solution.py:30
  137.1 36.1 %while.23 = (s32[]{:T(128)}, f32[3,6144]{1,0:T(4,128)S(1)}, f32[3,3,3,512]{3,0,2,1:T(4,128)S(1)}, s32[3,3,512]{2,1,0:T(4,128)S(1)}, s32[]{:T(128)}, /*index=5*/s32[]{:T(128)}) while((s32[]{:T(128)}, f32[3,6144]{1,0:T(4,128)S(1)}, f32[3,3,3,512]{3,0,2,1:T(4,128)S(1)}, s32[3,3,512]{2,1,0:T(4,128)S(1)}, s32[]{:T(128)}, ...), condition=%wide.region_5.6_spmd.clone, body=%wide.region_4.5_spmd.clone.sunk | while | flops 349212672 | bytes 221279 | solution.py:132
  137.2 11.9 %fusion.148 = f32[3,6144]{1,0:T(4,128)S(1)} fusion(s32[3,512]{1,0:T(4,128)S(1)} %dynamic-slice_bitcast_fusion.5, f32[3,6144]{1,0:T(4,128)S(1)} %get-tuple-element.226, pred[]{:T(512)S(6)} %compare.8, f32[1,3,3,512]{3,0,2,1:T(1,128)S(1)} %constant_dynamic-slice_fusion.2), kind=kOutput, calls=%fused_computation.12.clone.1 | convolution fusion | flops 349212672 | bytes 172033 | tf_op jit(solution)/shard_map/while/body/eval_jaxpr/cjb,jbp->cp/dot_general | solution.py:126
  149.1 11.9 %fusion.148 = f32[3,6144]{1,0:T(4,128)S(1)} fusion(s32[3,512]{1,0:T(4,128)S(1)} %dynamic-slice_bitcast_fusion.5, f32[3,6144]{1,0:T(4,128)S(1)} %get-tuple-element.226, pred[]{:T(512)S(6)} %compare.8, f32[1,3,3,512]{3,0,2,1:T(1,128)S(1)} %constant_dynamic-slice_fusion.2), kind=kOutput, calls=%fused_computation.12.clone.1 | convolution fusion | flops 349212672 | bytes 172033 | tf_op jit(solution)/shard_map/while/body/eval_jaxpr/cjb,jbp->cp/dot_general | solution.py:126
  161.1 11.9 %fusion.148 = f32[3,6144]{1,0:T(4,128)S(1)} fusion(s32[3,512]{1,0:T(4,128)S(1)} %dynamic-slice_bitcast_fusion.5, f32[3,6144]{1,0:T(4,128)S(1)} %get-tuple-element.226, pred[]{:T(512)S(6)} %compare.8, f32[1,3,3,512]{3,0,2,1:T(1,128)S(1)} %constant_dynamic-slice_fusion.2), kind=kOutput, calls=%fused_computation.12.clone.1 | convolution fusion | flops 349212672 | bytes 172033 | tf_op jit(solution)/shard_map/while/body/eval_jaxpr/cjb,jbp->cp/dot_general | solution.py:126
  173.2 3.1 reshape.111
  176.3 5.2 %collective-permute-start.5 = (f32[8,384]{1,0:T(8,128)S(1)}, f32[8,384]{1,0:T(8,128)S(1)}, u32[]{:S(2)}, u32[]{:S(2)}) collective-permute-start(f32[8,384]{1,0:T(8,128)S(1)} %get-tuple-element.139), channel_id=1, source_target_pairs={{0,1},{1,2},{2,3},{3,4},{4,5},{5,6},{6,7},{7,8},{8,9},{9,10},{10,1... | collective-permute-start | bytes 36872 | tf_op jit(solution)/shard_map/ppermute | solution.py:41
  181.5 1.3 collective-permute-start.6
  182.8 45.4 %pmin.7 = f32[]{:T(128)} all-reduce(f32[]{:T(128)} %get-tuple-element.142), channel_id=1, replica_groups=mesh['grp'=2,'patch'=16] {'grp','patch'}, use_global_device_ids=true, to_apply=%region_1.0 | all-reduce | flops 1 | bytes 8 | tf_op jit(solution)/shard_map/pmin | solution.py:155
  229.6 2.6 copy.80
  232.2 3.2 %mul.153 = f32[2064,3,128]{0,2,1:T(8,128)} broadcast(f32[2064,128]{0,1:T(8,128)} %copy.80), dimensions={0,2} | broadcast | bytes 4227072 | tf_op jit(solution)/shard_map/mul | solution.py:67
  235.3 3.2 copy.81
  238.5 3.2 %mul.144 = f32[2064,3,128]{0,2,1:T(8,128)} broadcast(f32[2064,128]{0,1:T(8,128)} %copy.69), dimensions={0,2} | broadcast | bytes 4227072 | tf_op jit(solution)/shard_map/mul | solution.py:59
  241.7 5.0 %copy.79 = f32[2064,384]{1,0:T(8,128)} copy(f32[2064,384]{0,1:T(8,128)} %bitcast.135) | data formatting | bytes 6340608 | tf_op jit(solution)/shard_map/mul | solution.py:59
  246.8 2.4 copy.100
  249.1 2.0 pad.18.clone
  251.2 3.5 %copy.78 = f32[2048,384]{1,0:T(8,128)} copy(f32[2048,384]{0,1:T(8,128)} %bitcast.136) | data formatting | bytes 6291456 | tf_op jit(solution)/shard_map/reshape | solution.py:137
  254.8 7.4 %fusion.69 = (bf16[2064,384]{1,0:T(8,128)(2,1)S(1)}, f32[2064,384]{1,0:T(8,128)S(1)}, f32[2064,384]{1,0:T(8,128)S(1)}) fusion(f32[]{:T(128)S(6)} %select_n.33, f32[2064,1408]{1,0:T(8,128)} %copy-done, f32[2064,384]{1,0:T(8,128)S(1)} %copy.81, f32[2064,384]{1,0:T(8,128)} %convolution_add_fusion.12, f32[2064,384]{1,0:T(8,128)} %copy.79, ...), kind=kLoop, calls=%fused_computation.107 | loop fusion | flops 8718336 | bytes 30117892 | tf_op jit(solution)/shard_map/convert_element_type | solution.py:167
  263.5 1.3 convolution_add_fusion.11
  266.9 1.4 convolution_add_fusion.10
  268.3 4.5 %convolution_add_fusion.9 = f32[2064,384]{1,0:T(8,128)} fusion(f32[2064,384]{1,0:T(8,128)S(1)} %convolution_add_fusion.10, bf16[2064,384]{1,0:T(8,128)(2,1)} %copy-done.4, bf16[5,384,384]{2,1,0:T(8,128)(2,1)} %param.17), kind=kOutput, calls=%fused_computation.41 | convolution fusion | flops 609490944 | bytes 8220672 | tf_op jit(solution)/shard_map/dot_general | solution.py:54
  272.9 8.3 %fusion.137 = (bf16[2064,384]{1,0:T(8,128)(2,1)}, f32[2064,384]{1,0:T(8,128)}, f32[2064,384]{1,0:T(8,128)}) fusion(f32[2064,384]{1,0:T(8,128)S(1)} %get-tuple-element.130, f32[]{:T(128)S(6)} %select_n.33, f32[2064,1408]{1,0:T(8,128)S(1)} %bitcast.131, pred[]{:T(512)S(6)} %eq.34, f32[2064,384]{1,0:T(8,128)S(1)} %copy.81, ...), kind=kOutput, calls=%fused_computation.189 | convolution fusion | flops 618209280 | bytes 28827652 | tf_op jit(solution)/shard_map/dot_general | solution.py:54
  281.2 2.8 fusion.38
  284.1 1.4 convolution_add_fusion.7
  285.9 1.3 convolution_add_fusion.6
  287.3 3.2 %convolution_add_fusion.5 = f32[2064,384]{1,0:T(8,128)} fusion(f32[2064,384]{1,0:T(8,128)S(1)} %convolution_add_fusion.6, bf16[2064,384]{1,0:T(8,128)(2,1)S(1)} %copy-done.5, bf16[5,384,384]{2,1,0:T(8,128)(2,1)S(1)} %copy-done.12), kind=kOutput, calls=%fused_computation.33 | convolution fusion | flops 609490944 | bytes 8220672 | tf_op jit(solution)/shard_map/dot_general | solution.py:54
  290.5 7.0 %fusion.136 = (bf16[2064,384]{1,0:T(8,128)(2,1)S(1)}, f32[2064,384]{1,0:T(8,128)}, f32[2064,384]{1,0:T(8,128)}, f32[2064,384]{1,0:T(8,128)}) fusion(f32[2064,384]{1,0:T(8,128)} %get-tuple-element.128, f32[]{:T(128)S(6)} %select_n.33, pred[]{:T(512)S(6)} %eq.34, f32[2064,384]{1,0:T(8,128)} %get-tuple-element.149, f32[2064,384]{1,0:T(8,128)S(1)} %get-tuple-element.130, ...), kind=kOutput, calls=%fused_computation.188 | convolution fusion | flops 618209280 | bytes 35168260 | tf_op jit(solution)/shard_map/dot_general | solution.py:54
  298.7 1.4 convolution_add_fusion.3
  300.1 1.4 convolution_add_fusion.2
  301.5 3.0 convolution_add_fusion.1
  305.5 6.0 %fusion.27 = f32[2064,384]{1,0:T(8,128)} fusion(f32[2064,384]{1,0:T(8,128)S(1)} %copy.81, f32[2064,384]{1,0:T(8,128)S(1)} %copy-done.3, f32[2064,384]{1,0:T(8,128)S(1)} %copy-done.1, f32[2064,384]{1,0:T(8,128)} %convolution_add_fusion.1, f32[]{:T(128)S(6)} %select_n.33, bf16[2064,384]{1,0:T(8,128)(2,1)S(1)} %get-tuple-element.125, ...), kind=kOutput, calls=%fused_computation.50 | convolution fusion | flops 615038976 | bytes 27242500 | tf_op jit(solution)/shard_map/dot_general | solution.py:54
  311.5 7.0 %fusion.29 = (f32[1,2048,384]{2,1,0:T(8,128)}, f32[1,2048,384]{2,1,0:T(8,128)}) fusion(f32[2064,384]{1,0:T(8,128)} %get-tuple-element.138, f32[2064,384]{1,0:T(8,128)} %fusion.27, pred[]{:T(512)S(6)} %eq.34, f32[]{:T(128)S(6)} %select_n.33, f32[2064,384]{1,0:T(8,128)} %get-tuple-element.126), kind=kLoop, calls=%fused_computation.56 | loop fusion | flops 3145728 | bytes 15728645 | tf_op jit(solution)/shard_map/broadcast_in_dim | solution.py:186
  (107 shorter events, 17.0 us)
Async XLA Ops:
  0.6 4.0 %copy-start.16 = (f32[1,2048,384]{2,1,0:T(8,128)S(1)}, f32[1,2048,384]{2,1,0:T(8,128)}, u32[]{:S(2)}) copy-start(f32[1,2048,384]{2,1,0:T(8,128)} %param.13) | copy-start | bytes 9437188
  4.7 3.0 copy-start.18
  7.7 2.0 copy-start.17
  7.7 3.1 copy-start.19
  9.7 8.2 %copy-start.15 = (f32[1,2048,384]{2,1,0:T(8,128)S(1)}, f32[1,2048,384]{2,1,0:T(8,128)}, u32[]{:S(2)}) copy-start(f32[1,2048,384]{2,1,0:T(8,128)} %param.12) | copy-start | bytes 9437188
  14.2 16.6 %collective-permute-start = (f32[8,1408]{1,0:T(8,128)}, f32[8,1408]{1,0:T(8,128)S(1)}, u32[]{:S(2)}, u32[]{:S(2)}) collective-permute-start(f32[8,1408]{1,0:T(8,128)} %get-tuple-element.134), channel_id=1, source_target_pairs={{0,1},{1,2},{2,3},{3,4},{4,5},{5,6},{6,7},{7,8},{8,9},{9,10},{10,1... | collective-permute-start | bytes 135176 | tf_op jit(solution)/shard_map/ppermute | solution.py:41
  16.6 14.2 %collective-permute-start.1 = (f32[8,1408]{1,0:T(8,128)}, f32[8,1408]{1,0:T(8,128)S(1)}, u32[]{:S(2)}, u32[]{:S(2)}) collective-permute-start(f32[8,1408]{1,0:T(8,128)} %get-tuple-element.135), channel_id=1, source_target_pairs={{1,0},{2,1},{3,2},{4,3},{5,4},{6,5},{7,6},{8,7},{9,8},{10,9},{11,1... | collective-permute-start | bytes 135176 | tf_op jit(solution)/shard_map/ppermute | solution.py:43
  20.3 3.4 %copy-start.22 = (s32[1,1,3,1536]{3,1,2,0:T(1,128)S(1)}, s32[1,1,3,1536]{3,1,2,0:T(1,128)}, u32[]{:S(2)}) copy-start(s32[1,1,3,1536]{3,1,2,0:T(1,128)} %param.18) | copy-start | bytes 55300
  20.3 3.5 %copy-start.23 = (f32[1,1,3,1536]{3,1,2,0:T(1,128)S(1)}, f32[1,1,3,1536]{3,1,2,0:T(1,128)}, u32[]{:S(2)}) copy-start(f32[1,1,3,1536]{3,1,2,0:T(1,128)} %param.19) | copy-start | bytes 55300
  36.3 8.4 %copy-start = (f32[2064,1408]{1,0:T(8,128)}, f32[2064,1408]{1,0:T(8,128)S(1)}, u32[]{:S(2)}) copy-start(f32[2064,1408]{1,0:T(8,128)S(1)} %pad_maximum_fusion) | copy-start | bytes 34873348
  36.3 2.5 copy-start.10
  51.4 3.4 %copy-start.9 = (f32[2064,384]{1,0:T(8,128)S(1)}, f32[2064,384]{1,0:T(8,128)}, u32[]{:S(2)}) copy-start(f32[2064,384]{1,0:T(8,128)} %fusion.46) | copy-start | bytes 9510916
  64.3 4.5 %copy-start.20 = (f32[3,9,3,512]{3,0,2,1:T(4,128)S(1)}, f32[3,9,3,512]{3,0,2,1:T(4,128)}, u32[]{:S(2)}) copy-start(f32[3,9,3,512]{3,0,2,1:T(4,128)} %custom-call.2) | copy-start | bytes 497668
  65.3 2.4 copy-start.21
  124.8 5.1 %collective-permute-start.2 = (bf16[9,3,1536]{2,1,0:T(4,128)(2,1)S(1)}, bf16[9,3,1536]{2,1,0:T(4,128)(2,1)S(1)}, u32[]{:S(2)}, u32[]{:S(2)}) collective-permute-start(bf16[9,3,1536]{2,1,0:T(4,128)(2,1)S(1)} %convert_element_type.48), channel_id=1, source_target_pairs={{0,16},{16,0},{1,17},{17,1},{2,18},{18,2},{3,19},{19,3},{4,20},{20... | collective-permute-start | bytes 248840 | tf_op jit(solution)/shard_map/ppermute | solution.py:24
  130.0 5.7 %collective-permute-start.4 = (bf16[9,1536]{1,0:T(8,128)(2,1)S(1)}, bf16[9,1536]{1,0:T(8,128)(2,1)S(1)}, u32[]{:S(2)}, u32[]{:S(2)}) collective-permute-start(bf16[9,1536]{1,0:T(8,128)(2,1)S(1)} %bitcast.144), channel_id=1, source_target_pairs={{1,0},{2,1},{3,2},{4,3},{5,4},{6,5},{7,6},{8,7},{9,8},{10,9},{11,1... | collective-permute-start | bytes 82952 | tf_op jit(solution)/shard_map/ppermute | solution.py:30
  131.3 5.2 %collective-permute-start.3 = (bf16[9,1536]{1,0:T(8,128)(2,1)S(1)}, bf16[9,1536]{1,0:T(8,128)(2,1)S(1)}, u32[]{:S(2)}, u32[]{:S(2)}) collective-permute-start(bf16[9,1536]{1,0:T(8,128)(2,1)S(1)} %bitcast.142), channel_id=1, source_target_pairs={{0,1},{1,2},{2,3},{3,4},{4,5},{5,6},{6,7},{7,8},{8,9},{9,10},{10,1... | collective-permute-start | bytes 82952 | tf_op jit(solution)/shard_map/ppermute | solution.py:30
  176.3 59.1 %copy-start.8 = (f32[3,2048,3]{2,1,0:T(8,128)}, f32[3,2048,3]{2,1,0:T(8,128)S(1)}, u32[]{:S(2)}) copy-start(f32[3,2048,3]{2,1,0:T(8,128)S(1)} %reshape.111) | copy-start | bytes 221188
  176.3 78.4 %collective-permute-start.5 = (f32[8,384]{1,0:T(8,128)S(1)}, f32[8,384]{1,0:T(8,128)S(1)}, u32[]{:S(2)}, u32[]{:S(2)}) collective-permute-start(f32[8,384]{1,0:T(8,128)S(1)} %get-tuple-element.139), channel_id=1, source_target_pairs={{0,1},{1,2},{2,3},{3,4},{4,5},{5,6},{6,7},{7,8},{8,9},{9,10},{10,1... | collective-permute-start | bytes 36872 | tf_op jit(solution)/shard_map/ppermute | solution.py:41
  181.5 73.2 %collective-permute-start.6 = (f32[8,384]{1,0:T(8,128)S(1)}, f32[8,384]{1,0:T(8,128)S(1)}, u32[]{:S(2)}, u32[]{:S(2)}) collective-permute-start(f32[8,384]{1,0:T(8,128)S(1)} %get-tuple-element.140), channel_id=1, source_target_pairs={{1,0},{2,1},{3,2},{4,3},{5,4},{6,5},{7,6},{8,7},{9,8},{10,9},{11,1... | collective-permute-start | bytes 36872 | tf_op jit(solution)/shard_map/ppermute | solution.py:43
  254.7 7.5 %copy-start.11 = (bf16[5,384,384]{2,1,0:T(8,128)(2,1)S(1)}, bf16[5,384,384]{2,1,0:T(8,128)(2,1)}, u32[]{:S(2)}) copy-start(bf16[5,384,384]{2,1,0:T(8,128)(2,1)} %param.17) | copy-start | bytes 4423684
  254.7 10.1 %slice-start = ((s8[11624448]{0:T(1024)(128)(4,1)}), s8[4194304]{0:T(1024)(128)(4,1)S(1)}, s32[]{:S(2)}) async-start(s8[11624448]{0:T(1024)(128)(4,1)} %bitcast.130), calls=%async_computation | async-start | bytes 8388608
  254.7 11.1 %slice-start.1 = ((s8[11624448]{0:T(1024)(128)(4,1)}), s8[4194304]{0:T(1024)(128)(4,1)S(1)}, s32[]{:S(2)}) async-start(s8[11624448]{0:T(1024)(128)(4,1)} %bitcast.130), calls=%async_computation.1 | async-start | bytes 8388608
  262.2 2.6 copy-start.4
  262.2 10.7 %copy-start.2 = (f32[2064,384]{1,0:T(8,128)}, f32[2064,384]{1,0:T(8,128)S(1)}, u32[]{:S(2)}) copy-start(f32[2064,384]{1,0:T(8,128)S(1)} %get-tuple-element.131) | copy-start | bytes 9510916
  262.2 4.7 %slice-start.2 = ((s8[11624448]{0:T(1024)(128)(4,1)}), s8[3235840]{0:T(1024)(128)(4,1)S(1)}, s32[]{:S(2)}) async-start(s8[11624448]{0:T(1024)(128)(4,1)} %bitcast.130), calls=%async_computation.2 | async-start | bytes 6471680
  268.3 4.6 %copy-start.1 = (f32[2064,384]{1,0:T(8,128)S(1)}, f32[2064,384]{1,0:T(8,128)}, u32[]{:S(2)}) copy-start(f32[2064,384]{1,0:T(8,128)} %copy.79) | copy-start | bytes 9510916
  281.2 2.9 copy-start.5
  281.2 2.9 copy-start.12
  284.1 1.9 copy-start.6
  287.3 3.2 %copy-start.3 = (f32[2064,384]{1,0:T(8,128)S(1)}, f32[2064,384]{1,0:T(8,128)}, u32[]{:S(2)}) copy-start(f32[2064,384]{1,0:T(8,128)} %copy-done.2) | copy-start | bytes 9510916
  287.3 3.2 %copy-start.13 = (bf16[5,384,384]{2,1,0:T(8,128)(2,1)S(1)}, bf16[5,384,384]{2,1,0:T(8,128)(2,1)}, u32[]{:S(2)}) copy-start(bf16[5,384,384]{2,1,0:T(8,128)(2,1)} %param.17) | copy-start | bytes 4423684
  301.5 3.1 copy-start.7
  301.5 4.0 %copy-start.14 = (f32[2064,384]{1,0:T(8,128)S(1)}, f32[2064,384]{1,0:T(8,128)}, u32[]{:S(2)}) copy-start(f32[2064,384]{1,0:T(8,128)} %get-tuple-element.150) | copy-start | bytes 9510916
where the time goes:
time: 325 us; the launch traced here: 319 us
  matrix products  147 us (45%)
  local copies, waits for them, and re-layouts  73.8 us (23%)
  blocking collectives  45.4 us (14%)
  other arithmetic  26.6 us (8%)
  starting transfers between devices  18.2 us (6%)
  waiting for transfers between devices  3.47 us (1%)
    dot_general x20, matrix products, band_force(): jnp.dot(padded[band_index:band_index + row_count], stiff_bands[band_index...  61.1 us
    dot_general x3, matrix products, pick_block(): jnp.einsum('qp,jbp->qjb', edge_matrix, selector(table_block), precision=l...  50.6 us
    pmin x1, blocking collectives, per_device(): base_step = COURANT * lax.pmin(local_limit, ('grp', 'patch'))  45.4 us
    dot_general x3, matrix products, spread_block(): jnp.einsum('cjb,jbp->cp', force_block, selector(table_block), precision=l...  35.8 us
    unnamed x64, local copies, waits for them, and re-layouts  23.2 us
    mul x2, local copies, waits for them, and re-layouts, band_force(): summed.reshape(row_count, 3, POINTS) * thickness[:, None, :]  8.23 us
    ppermute x2, starting transfers between devices, padded_2(): lax.ppermute(tail, axis, [(i, (i + 1) % count) for i in range(ends)])  7.6 us
    convert_element_type x1, other arithmetic, wide_force(): padded = jnp.pad(current.astype(jnp.bfloat16), ((REACH, REACH), (0, 0)))  7.42 us
  transfers between devices with their start and end apart: 7, of which 2 were waited for; matrix products, arithmetic and copies ran while one was open for 12% of the time, Pallas kernels for 0%

commit v1 on v0

v1 whole, which is shorter than its diff:
```python
import functools

import jax
import jax.numpy as jnp
from jax import lax
from jax.experimental import pallas as pl
from jax.experimental.pallas import tpu as pltpu
from jax.sharding import PartitionSpec as P

POINTS = 128
REACH = 2
SUBSTEPS = 4
EDGE = 3
COURANT = 0.4
HALO = REACH * SUBSTEPS
BASE = 2 * HALO
LANES = 128
MESH = pl.DeviceIdType.MESH


def row_chunk(rows, most):
    tiles = rows // 8
    return 8 * max(d for d in range(1, tiles + 1) if tiles % d == 0 and 8 * d <= most)


def iota(shape, dim):
    return lax.broadcasted_iota(jnp.int32, shape, dim)


def kernel(
    n_grp,
    n_patch,
    disp_hbm,
    vel_hbm,
    ext_hbm,
    mass_hbm,
    thick_hbm,
    band_hbm,
    pts_ref,
    wts_ref,
    disp_out,
    vel_out,
    xa,
    xb,
    vel,
    frc,
    ext,
    mass,
    thick,
    band,
    table,
    sent,
    got,
    spread,
    peak,
    load_sem,
    halo_send,
    halo_recv,
    trace_send,
    trace_recv,
    far_send,
    far_recv,
    peak_send,
    peak_recv,
    out_sem,
):
    g = lax.axis_index("grp")
    p = lax.axis_index("patch")
    rows = disp_hbm.shape[1]
    width = disp_hbm.shape[2]
    slots = pts_ref.shape[3]
    total = rows + 2 * BASE
    own = pl.ds(BASE, rows)
    has_low = p > 0
    has_high = p < n_patch - 1

    loads = [
        pltpu.make_async_copy(mass_hbm.at[0], mass.at[own], load_sem.at[0]),
        pltpu.make_async_copy(thick_hbm.at[0], thick.at[own], load_sem.at[1]),
        pltpu.make_async_copy(band_hbm, band, load_sem.at[2]),
        pltpu.make_async_copy(disp_hbm.at[0], xa.at[own], load_sem.at[3]),
        pltpu.make_async_copy(vel_hbm.at[0], vel.at[own], load_sem.at[4]),
        pltpu.make_async_copy(ext_hbm.at[0], ext.at[own], load_sem.at[5]),
    ]
    for load in loads:
        load.start()

    def halo_copy(k, up):
        source, target = ((disp_hbm, xa), (vel_hbm, vel), (mass_hbm, mass), (thick_hbm, thick))[k]
        if up:
            src = source.at[0, pl.ds(rows - HALO, HALO)]
            dst = target.at[pl.ds(BASE - HALO, HALO)]
            to = p + 1
        else:
            src = source.at[0, pl.ds(0, HALO)]
            dst = target.at[pl.ds(BASE + rows, HALO)]
            to = p - 1
        return pltpu.make_async_remote_copy(
            src_ref=src,
            dst_ref=dst,
            send_sem=halo_send.at[k, int(up)],
            recv_sem=halo_recv.at[k, int(up)],
            device_id={"grp": g, "patch": to},
            device_id_type=MESH,
        )

    @pl.when(has_high)
    def _():
        for k in range(4):
            halo_copy(k, True).start()

    @pl.when(has_low)
    def _():
        for k in range(4):
            halo_copy(k, False).start()

    for buf in (xa, xb, vel, frc, ext, mass, thick):
        zero = jnp.zeros((HALO, buf.shape[1]), jnp.float32)
        buf[pl.ds(0, HALO), :] = zero
        buf[pl.ds(total - HALO, HALO), :] = zero

    @pl.when(p == 0)
    def _():
        for buf in (xa, vel, ext, mass, thick):
            buf[pl.ds(BASE - HALO, HALO), :] = jnp.zeros((HALO, buf.shape[1]), jnp.float32)
        got[0] = jnp.zeros(got.shape[1:], jnp.float32)

    @pl.when(p == n_patch - 1)
    def _():
        for buf in (xa, vel, ext, mass, thick):
            buf[pl.ds(BASE + rows, HALO), :] = jnp.zeros((HALO, buf.shape[1]), jnp.float32)
        got[2] = jnp.zeros(got.shape[1:], jnp.float32)

    loads[0].wait()
    loads[1].wait()
    peak_rows = row_chunk(rows, 256)

    def peak_step(i, high):
        at = pl.ds(pl.multiple_of(BASE + i * peak_rows, 8), peak_rows)
        product = (mass[at, :] * thick[at, :]).reshape(peak_rows // 8, 8, LANES)
        return jnp.maximum(high, jnp.max(product, axis=0))

    peak[0] = lax.fori_loop(
        0, rows // peak_rows, peak_step, jnp.zeros((8, LANES), jnp.float32)
    )
    count = n_grp * n_patch
    me = g * n_patch + p

    def peak_start(k, carry):
        to = (me + k) % count
        pltpu.make_async_remote_copy(
            src_ref=peak.at[0],
            dst_ref=peak.at[k],
            send_sem=peak_send,
            recv_sem=peak_recv,
            device_id={"grp": to // n_patch, "patch": to % n_patch},
            device_id_type=MESH,
        ).start()
        return carry

    lax.fori_loop(1, count, peak_start, 0)

    def force(src, at, length):
        around = src[pl.ds(pl.multiple_of(at - 8, 8), length + 16), :]
        parts = [
            around[8 + b - REACH : 8 + b - REACH + length].astype(jnp.bfloat16)
            for b in range(2 * REACH + 1)
        ]
        summed = jnp.dot(
            jnp.concatenate(parts, axis=1), band[...], preferred_element_type=jnp.float32
        )
        t = thick[pl.ds(at, length), :]
        return summed * jnp.concatenate([t, t, t], axis=1)

    loads[2].wait()
    loads[3].wait()

    @pl.when(has_low)
    def _():
        for k in range(4):
            halo_copy(k, True).wait_recv()

    @pl.when(has_high)
    def _():
        for k in range(4):
            halo_copy(k, False).wait_recv()

    wide_chunk = row_chunk(rows + 2 * HALO, 352)
    wide_count = (rows + 2 * HALO) // wide_chunk

    def first_force(i, carry):
        at = pl.multiple_of(HALO + i * wide_chunk, 8)
        frc[pl.ds(at, wide_chunk), :] = force(xa, at, wide_chunk)
        return carry

    lax.fori_loop(0, wide_count, first_force, 0)
    loads[4].wait()

    blocks = rows // LANES

    def edge_mix(at, length):
        return xa[pl.ds(at, length), :] + 0.5 * (
            vel[pl.ds(at, length), :] + frc[pl.ds(at, length), :]
        )

    key = iota((16, width), 0)
    lane = iota((16, width), 1)
    pick = jnp.where(
        (key % 4 == lane // POINTS) & (key // 4 == lane % POINTS), 1.0, 0.0
    ).astype(jnp.bfloat16)

    def table_step(h, carry):
        at = pl.multiple_of(BASE + h * LANES, 8)
        mix = edge_mix(at, LANES).astype(jnp.bfloat16)
        table[pl.ds(pl.multiple_of(h * 16, 16), 16), :] = lax.dot_general(
            pick, mix, (((1,), (1,)), ((), ())), preferred_element_type=jnp.float32
        ).astype(jnp.bfloat16)
        return carry

    lax.fori_loop(0, blocks, table_step, 0)

    slot_chunk = min(512, slots)
    slot_count = slots // slot_chunk
    key_col = iota((16, slot_chunk), 0) // 4
    low_col = iota((LANES, slot_chunk), 0)
    out_row = iota((8, 16), 0) % 4
    in_key = iota((8, 16), 1)
    fold = jnp.where((in_key % 4 == out_row) & (out_row < 3), 1.0, 0.0).astype(jnp.bfloat16)

    def slot_split(j, at):
        entry = pts_ref[0, 0, pl.ds(j, 1), at]
        row = entry // EDGE
        return row // LANES, row % LANES, entry - row * EDGE

    def trace_copy(j):
        return pltpu.make_async_remote_copy(
            src_ref=sent.at[j],
            dst_ref=got.at[2 - j],
            send_sem=trace_send.at[j],
            recv_sem=trace_recv.at[2 - j],
            device_id={"grp": 1 - g, "patch": p + (j - 1)},
            device_id_type=MESH,
        )

    exists = (has_low, None, has_high)

    def guarded(cond, run):
        if cond is None:
            run()
        else:
            pl.when(cond)(run)

    for j in range(3):

        def gather_step(c, carry, j=j):
            at = pl.ds(pl.multiple_of(c * slot_chunk, LANES), slot_chunk)
            high, low, point = slot_split(j, at)
            hot = jnp.where(low_col == low, 1.0, 0.0).astype(jnp.bfloat16)
            found = jnp.dot(table[...], hot, preferred_element_type=jnp.float32)
            total_found = jnp.zeros((16, slot_chunk), jnp.float32)
            for h in range(blocks):
                total_found = jnp.where(high == h, found[h * 16 : h * 16 + 16], total_found)
            total_found = jnp.where(key_col == point, total_found, 0.0)
            sent[j, :, at] = jnp.dot(
                fold, total_found.astype(jnp.bfloat16), preferred_element_type=jnp.float32
            )
            return carry

        lax.fori_loop(0, slot_count, gather_step, 0)
        guarded(exists[j], lambda j=j: trace_copy(j).start())

    spread[...] = jnp.zeros(spread.shape, jnp.float32)
    one_row = jnp.where(iota((8, slot_chunk), 0) % 4 == 3, 1.0, 0.0)
    for j in (1, 0, 2):
        guarded(exists[j], lambda j=j: trace_copy(2 - j).wait_recv())
        present = 1.0 if exists[j] is None else jnp.where(exists[j], 1.0, 0.0)

        def spread_step(c, carry, j=j, present=present):
            at = pl.ds(pl.multiple_of(c * slot_chunk, LANES), slot_chunk)
            high, low, point = slot_split(j, at)
            weight = wts_ref[0, 0, pl.ds(j, 1), at] * present
            value = (got[j, :, at] + one_row) * weight
            value = jnp.where(key_col == point, jnp.concatenate([value, value], axis=0), 0.0)
            coarse = value.astype(jnp.bfloat16).astype(jnp.float32)
            fine = value - coarse
            pieces = [jnp.where(high == h, coarse, 0.0).astype(jnp.bfloat16) for h in range(blocks)]
            pieces += [jnp.where(high == h, fine, 0.0).astype(jnp.bfloat16) for h in range(blocks)]
            hot = jnp.where(low_col == low, 1.0, 0.0).astype(jnp.bfloat16)
            spread[...] += lax.dot_general(
                jnp.concatenate(pieces, axis=0),
                hot,
                (((1,), (1,)), ((), ())),
                preferred_element_type=jnp.float32,
            )
            return carry

        lax.fori_loop(0, slot_count, spread_step, 0)

    loads[5].wait()
    key2 = iota((LANES, 2 * width), 0)
    lane2 = iota((LANES, 2 * width), 1)
    place_key = key2 % 16
    comp = place_key % 4
    hit = comp == jnp.where(lane2 < width, lane2 // POINTS, 3)
    place = jnp.where(
        hit & (place_key // 4 == lane2 % POINTS) & (key2 < 48), 1.0, 0.0
    ).astype(jnp.bfloat16)

    def couple_step(i, carry):
        h = (i + blocks - 1) % blocks
        summed = (
            spread[pl.ds(pl.multiple_of(h * 16, 16), 16), :]
            + spread[pl.ds(pl.multiple_of((blocks + h) * 16, 16), 16), :]
        )
        first = summed.astype(jnp.bfloat16).astype(jnp.float32)
        rest = summed - first
        second = rest.astype(jnp.bfloat16).astype(jnp.float32)
        stack = jnp.concatenate(
            [first, second, rest - second, jnp.zeros((LANES - 48, LANES), jnp.float32)], axis=0
        )
        placed = jnp.dot(
            stack.T.astype(jnp.bfloat16), place, preferred_element_type=jnp.float32
        )
        at = pl.multiple_of(BASE + h * LANES, 8)
        mix = edge_mix(at, LANES)
        ext[pl.ds(at, LANES), :] += placed[:, :width] - mix * placed[:, width:]
        return carry

    def far_copy(up):
        if up:
            src, dst, to = pl.ds(BASE + rows - HALO, HALO), pl.ds(BASE - HALO, HALO), p + 1
        else:
            src, dst, to = pl.ds(BASE, HALO), pl.ds(BASE + rows, HALO), p - 1
        return pltpu.make_async_remote_copy(
            src_ref=ext.at[src],
            dst_ref=ext.at[dst],
            send_sem=far_send.at[int(up)],
            recv_sem=far_recv.at[int(up)],
            device_id={"grp": g, "patch": to},
            device_id_type=MESH,
        )

    fine_group = g == 1
    lax.fori_loop(0, 2, couple_step, 0)
    pl.when(fine_group & has_high)(lambda: far_copy(True).start())
    pl.when(fine_group & has_low)(lambda: far_copy(False).start())
    lax.fori_loop(2, blocks, couple_step, 0)

    arrived = peak.at[pl.ds(1, count - 1)]
    pltpu.make_async_copy(arrived, arrived, peak_recv).wait()
    top = jnp.max(jnp.max(peak[...], axis=0), axis=(0, 1), keepdims=True)
    base_step = COURANT * (1.0 / jnp.sqrt(top))
    size = jnp.where(g == 0, SUBSTEPS * base_step, base_step)

    pl.when(fine_group & has_low)(lambda: far_copy(True).wait_recv())
    pl.when(fine_group & has_high)(lambda: far_copy(False).wait_recv())

    def advance(src, dst, at, length, inner):
        m = mass[pl.ds(at, length), :]
        moved = vel[pl.ds(at, length), :] + size * (
            jnp.concatenate([m, m, m], axis=1) * (ext[pl.ds(at, length), :] - inner)
        )
        vel[pl.ds(at, length), :] = moved
        dst[pl.ds(at, length), :] = src[pl.ds(at, length), :] + size * moved

    plain_chunk = row_chunk(rows, 256)
    plain_count = rows // plain_chunk

    def outputs(src, i):
        at = pl.multiple_of(i * plain_chunk, 8)
        here = pl.ds(BASE + at, plain_chunk)
        there = pl.ds(at, plain_chunk)
        return (
            pltpu.make_async_copy(src.at[here], disp_out.at[0, there], out_sem.at[0, i]),
            pltpu.make_async_copy(vel.at[here], vel_out.at[0, there], out_sem.at[1, i]),
        )

    def put(src, i):
        for copy in outputs(src, i):
            copy.start()

    @pl.when(g == 0)
    def _():
        def step(i, carry):
            at = pl.multiple_of(BASE + i * plain_chunk, 8)
            advance(xa, xb, at, plain_chunk, frc[pl.ds(at, plain_chunk), :])
            put(xb, i)
            return carry

        lax.fori_loop(0, plain_count, step, 0)

    @pl.when(fine_group)
    def _():
        def step(i, carry):
            at = pl.multiple_of(HALO + i * wide_chunk, 8)
            advance(xa, xb, at, wide_chunk, frc[pl.ds(at, wide_chunk), :])
            return carry

        lax.fori_loop(0, wide_count, step, 0)
        src, dst = xb, xa
        for _ in range(SUBSTEPS - 2):

            def step(i, carry, src=src, dst=dst):
                at = pl.multiple_of(HALO + i * wide_chunk, 8)
                advance(src, dst, at, wide_chunk, force(src, at, wide_chunk))
                return carry

            lax.fori_loop(0, wide_count, step, 0)
            src, dst = dst, src

        def step(i, carry):
            at = pl.multiple_of(BASE + i * plain_chunk, 8)
            advance(src, dst, at, plain_chunk, force(src, at, plain_chunk))
            put(dst, i)
            return carry

        lax.fori_loop(0, plain_count, step, 0)

    last = (xb, xa)[(SUBSTEPS - 1) % 2]

    def drain(src):
        def step(i, carry):
            for copy in outputs(src, i):
                copy.wait()
            return carry

        lax.fori_loop(0, plain_count, step, 0)

    pl.when(g == 0)(lambda: drain(xb))
    pl.when(fine_group)(lambda: drain(last))

    @pl.when(has_high)
    def _():
        for k in range(4):
            halo_copy(k, True).wait_send()

    @pl.when(has_low)
    def _():
        for k in range(4):
            halo_copy(k, False).wait_send()

    for j in range(3):
        guarded(exists[j], lambda j=j: trace_copy(j).wait_send())
    pl.when(fine_group & has_high)(lambda: far_copy(True).wait_send())
    pl.when(fine_group & has_low)(lambda: far_copy(False).wait_send())
    pltpu.make_async_copy(arrived, arrived, peak_send).wait()


def per_device(
    n_grp,
    n_patch,
    displace,
    velocity,
    ext_force,
    inv_mass,
    thickness,
    stiff_bands,
    pair_points,
    pair_weights,
):
    rows, width = displace.shape[1:]
    slots = pair_points.shape[3]
    total = rows + 2 * BASE
    blocks = rows // LANES
    bands = stiff_bands.reshape(stiff_bands.shape[0] * width, width)
    anywhere = pl.BlockSpec(memory_space=pl.ANY)
    vmem = pl.BlockSpec(memory_space=pltpu.VMEM)
    wide = pltpu.VMEM((total, width), jnp.float32)
    slim = pltpu.VMEM((total, POINTS), jnp.float32)
    dma = pltpu.SemaphoreType.DMA
    plain_count = rows // row_chunk(rows, 256)
    return pl.pallas_call(
        functools.partial(kernel, n_grp, n_patch),
        out_shape=[jax.ShapeDtypeStruct(displace.shape, jnp.float32)] * 2,
        in_specs=[anywhere] * 6 + [vmem] * 2,
        out_specs=[anywhere] * 2,
        scratch_shapes=[
            wide,
            wide,
            wide,
            wide,
            wide,
            slim,
            slim,
            pltpu.VMEM(bands.shape, jnp.bfloat16),
            pltpu.VMEM((blocks * 16, LANES), jnp.bfloat16),
            pltpu.VMEM((3, 8, slots), jnp.float32),
            pltpu.VMEM((3, 8, slots), jnp.float32),
            pltpu.VMEM((blocks * 32, LANES), jnp.float32),
            pltpu.VMEM((n_grp * n_patch, 8, LANES), jnp.float32),
            dma((6,)),
            dma((4, 2)),
            dma((4, 2)),
            dma((3,)),
            dma((3,)),
            dma((2,)),
            dma((2,)),
            dma,
            dma,
            dma((2, plain_count)),
        ],
        compiler_params=pltpu.CompilerParams(
            has_side_effects=True, vmem_limit_bytes=56 * 1024 * 1024
        ),
        name="shell_step",
    )(displace, velocity, ext_force, inv_mass, thickness, bands, pair_points, pair_weights)


def solution(mesh):
    return jax.shard_map(
        functools.partial(per_device, mesh.shape["grp"], mesh.shape["patch"]),
        mesh=mesh,
        in_specs=(
            P("grp", "patch", None),
            P("grp", "patch", None),
            P("grp", "patch", None),
            P("grp", "patch", None),
            P("grp", "patch", None),
            P(),
            P("grp", "patch", None, None),
            P("grp", "patch", None, None),
        ),
        out_specs=(P("grp", "patch", None), P("grp", "patch", None)),
        check_vma=False,
    )
```

time: 325 us -> 61.1 us (0.19)
  the two profiles are of different devices: /device:TPU:0 before, /device:TPU:15 now
where the time goes in v1:
time: 61.1 us; the launch traced here: 60.8 us
  Pallas kernels  51.9 us (85%)
  local copies, waits for them, and re-layouts  8.25 us (14%)
  between operations  0.65 us (1%)
    pallas_call x1, Pallas kernels, per_device(): pl.pallas_call(functools.partial(kernel, n_grp, n_patch), out_shape=[jax....  51.9 us
    unnamed x6, local copies, waits for them, and re-layouts  8.25 us

profile of v1, /device:TPU:15, one launch (start us, length us, event | category | flops | bytes accessed | tf_op | source)
XLA Modules:
  0.0 60.8 jit_solution(14516515194833763368)
XLA Ops:
  0.6 1.3 %copy.10.pts_ref = s32[1,1,3,1536]{3,2,1,0:T(4,128)} copy(s32[1,1,3,1536]{3,1,2,0:T(1,128)} %param.14) | data formatting | bytes 36864 | tf_op args[6]
  2.0 1.3 %copy.11.wts_ref = f32[1,1,3,1536]{3,2,1,0:T(4,128)} copy(f32[1,1,3,1536]{3,1,2,0:T(1,128)} %param.15) | data formatting | bytes 36864 | tf_op args[7]
  3.3 51.9 %shell_step.1 = (f32[1,2048,384]{2,1,0:T(8,128)}, f32[1,2048,384]{2,1,0:T(8,128)}) custom-call(f32[1,2048,384]{2,1,0:T(8,128)} %disp_hbm.1, f32[1,2048,384]{2,1,0:T(8,128)} %vel_hbm.1, f32[1,2048,384]{2,1,0:T(8,128)} %ext_hbm.1, f32[1,2048,128]{2,1,0:T(8,128)} %mass_hbm.1, f32[1,2048,128]{2,1,0:T(8,128)} %thick_hbm.1, bf16[1920,384]{1,0:T(8,128)(2,1)} %bitcast.1, ...), custom_call_target="tpu_custom_call" | custom-call | tf_op jit(solution)/shard_map/shell_step/pallas_call | solution.py:472
  55.2 0.0 copy-start
  55.2 3.9 %copy.14 = f32[1,2048,384]{2,1,0:T(8,128)} copy(f32[1,2048,384]{2,1,0:T(8,128)} %get-tuple-element.4) | data formatting | bytes 6291456
  59.1 0.0 copy-done
  59.1 1.7 %copy.15 = f32[1,2048,384]{2,1,0:T(8,128)} copy(f32[1,2048,384]{2,1,0:T(8,128)S(1)} %copy-done) | data formatting | bytes 6291456
Async XLA Ops:
  55.2 3.9 %copy-start = (f32[1,2048,384]{2,1,0:T(8,128)S(1)}, f32[1,2048,384]{2,1,0:T(8,128)}, u32[]{:S(2)}) copy-start(f32[1,2048,384]{2,1,0:T(8,128)} %get-tuple-element.5) | copy-start | bytes 9437188

commit v2 on v1

--- a/solution.py
+++ b/solution.py
@@ -25,6 +25,28 @@
 
 def iota(shape, dim):
     return lax.broadcasted_iota(jnp.int32, shape, dim)
+
+
+def force(src, band, thick, at, length):
+    around = src[pl.ds(pl.multiple_of(at - 8, 8), length + 16), :]
+    parts = [
+        around[8 + b - REACH : 8 + b - REACH + length].astype(jnp.bfloat16)
+        for b in range(2 * REACH + 1)
+    ]
+    summed = jnp.dot(
+        jnp.concatenate(parts, axis=1), band[...], preferred_element_type=jnp.float32
+    )
+    t = thick[pl.ds(at, length), :]
+    return summed * jnp.concatenate([t, t, t], axis=1)
+
+
+def advance(size, src, dst, vel, vel_dst, ext, mass, at, length, inner):
+    m = mass[pl.ds(at, length), :]
+    moved = vel[pl.ds(at, length), :] + size * (
+        jnp.concatenate([m, m, m], axis=1) * (ext[pl.ds(at, length), :] - inner)
+    )
+    vel_dst[pl.ds(at, length), :] = moved
+    dst[pl.ds(at, length), :] = src[pl.ds(at, length), :] + size * moved
 
 
 def kernel(
@@ -38,15 +60,14 @@
     band_hbm,
     pts_ref,
     wts_ref,
-    disp_out,
-    vel_out,
-    xa,
     xb,
     vel,
-    frc,
     ext,
     mass,
     thick,
+    size_out,
+    xa,
+    frc,
     band,
     table,
     sent,
@@ -62,13 +83,12 @@
     far_recv,
     peak_send,
     peak_recv,
-    out_sem,
 ):
     g = lax.axis_index("grp")
     p = lax.axis_index("patch")
     rows = disp_hbm.shape[1]
     width = disp_hbm.shape[2]
-    slots = pts_ref.shape[3]
+    slots = pts_ref.shape[2]
     total = rows + 2 * BASE
     own = pl.ds(BASE, rows)
     has_low = p > 0
@@ -160,18 +180,6 @@
 
     lax.fori_loop(1, count, peak_start, 0)
 
-    def force(src, at, length):
-        around = src[pl.ds(pl.multiple_of(at - 8, 8), length + 16), :]
-        parts = [
-            around[8 + b - REACH : 8 + b - REACH + length].astype(jnp.bfloat16)
-            for b in range(2 * REACH + 1)
-        ]
-        summed = jnp.dot(
-            jnp.concatenate(parts, axis=1), band[...], preferred_element_type=jnp.float32
-        )
-        t = thick[pl.ds(at, length), :]
-        return summed * jnp.concatenate([t, t, t], axis=1)
-
     loads[2].wait()
     loads[3].wait()
 
@@ -190,7 +198,7 @@
 
     def first_force(i, carry):
         at = pl.multiple_of(HALO + i * wide_chunk, 8)
-        frc[pl.ds(at, wide_chunk), :] = force(xa, at, wide_chunk)
+        frc[pl.ds(at, wide_chunk), :] = force(xa, band, thick, at, wide_chunk)
         return carry
 
     lax.fori_loop(0, wide_count, first_force, 0)
@@ -228,7 +236,7 @@
     fold = jnp.where((in_key % 4 == out_row) & (out_row < 3), 1.0, 0.0).astype(jnp.bfloat16)
 
     def slot_split(j, at):
-        entry = pts_ref[0, 0, pl.ds(j, 1), at]
+        entry = pts_ref[j, :, at]
         row = entry // EDGE
         return row // LANES, row % LANES, entry - row * EDGE
 
@@ -278,7 +286,7 @@
         def spread_step(c, carry, j=j, present=present):
             at = pl.ds(pl.multiple_of(c * slot_chunk, LANES), slot_chunk)
             high, low, point = slot_split(j, at)
-            weight = wts_ref[0, 0, pl.ds(j, 1), at] * present
+            weight = wts_ref[j, :, at] * present
             value = (got[j, :, at] + one_row) * weight
             value = jnp.where(key_col == point, jnp.concatenate([value, value], axis=0), 0.0)
             coarse = value.astype(jnp.bfloat16).astype(jnp.float32)
@@ -355,18 +363,43 @@
     pl.when(fine_group & has_low)(lambda: far_copy(True).wait_recv())
     pl.when(fine_group & has_high)(lambda: far_copy(False).wait_recv())
 
-    def advance(src, dst, at, length, inner):
-        m = mass[pl.ds(at, length), :]
-        moved = vel[pl.ds(at, length), :] + size * (
-            jnp.concatenate([m, m, m], axis=1) * (ext[pl.ds(at, length), :] - inner)
-        )
-        vel[pl.ds(at, length), :] = moved
-        dst[pl.ds(at, length), :] = src[pl.ds(at, length), :] + size * moved
-
+    def step(i, carry):
+        at = pl.multiple_of(HALO + i * wide_chunk, 8)
+        advance(size, xa, xb, vel, vel, ext, mass, at, wide_chunk, frc[pl.ds(at, wide_chunk), :])
+        return carry
+
+    lax.fori_loop(0, wide_count, step, 0)
+    size_out[...] = jnp.broadcast_to(size, size_out.shape)
+
+    @pl.when(has_high)
+    def _():
+        for k in range(4):
+            halo_copy(k, True).wait_send()
+
+    @pl.when(has_low)
+    def _():
+        for k in range(4):
+            halo_copy(k, False).wait_send()
+
+    for j in range(3):
+        guarded(exists[j], lambda j=j: trace_copy(j).wait_send())
+    pl.when(fine_group & has_high)(lambda: far_copy(True).wait_send())
+    pl.when(fine_group & has_low)(lambda: far_copy(False).wait_send())
+    pltpu.make_async_copy(arrived, arrived, peak_send).wait()
+
+
+def steps_kernel(
+    xb, vel, ext, mass, thick, size_ref, band_hbm, disp_out, vel_out, xa, xc, held, band, load_sem, out_sem
+):
+    g = lax.axis_index("grp")
+    rows = disp_out.shape[1]
+    total = rows + 2 * BASE
+    wide_chunk = row_chunk(rows + 2 * HALO, 352)
+    wide_count = (rows + 2 * HALO) // wide_chunk
     plain_chunk = row_chunk(rows, 256)
     plain_count = rows // plain_chunk
 
-    def outputs(src, i):
+    def outputs(src, vel, i):
         at = pl.multiple_of(i * plain_chunk, 8)
         here = pl.ds(BASE + at, plain_chunk)
         there = pl.ds(at, plain_chunk)
@@ -375,75 +408,55 @@
             pltpu.make_async_copy(vel.at[here], vel_out.at[0, there], out_sem.at[1, i]),
         )
 
-    def put(src, i):
-        for copy in outputs(src, i):
+    def put(src, vel, i):
+        for copy in outputs(src, vel, i):
             copy.start()
 
-    @pl.when(g == 0)
-    def _():
+    def drain(src, vel):
         def step(i, carry):
-            at = pl.multiple_of(BASE + i * plain_chunk, 8)
-            advance(xa, xb, at, plain_chunk, frc[pl.ds(at, plain_chunk), :])
-            put(xb, i)
-            return carry
-
-        lax.fori_loop(0, plain_count, step, 0)
-
-    @pl.when(fine_group)
-    def _():
-        def step(i, carry):
-            at = pl.multiple_of(HALO + i * wide_chunk, 8)
-            advance(xa, xb, at, wide_chunk, frc[pl.ds(at, wide_chunk), :])
-            return carry
-
-        lax.fori_loop(0, wide_count, step, 0)
-        src, dst = xb, xa
-        for _ in range(SUBSTEPS - 2):
-
-            def step(i, carry, src=src, dst=dst):
-                at = pl.multiple_of(HALO + i * wide_chunk, 8)
-                advance(src, dst, at, wide_chunk, force(src, at, wide_chunk))
-                return carry
-
-            lax.fori_loop(0, wide_count, step, 0)
-            src, dst = dst, src
-
-        def step(i, carry):
-            at = pl.multiple_of(BASE + i * plain_chunk, 8)
-            advance(src, dst, at, plain_chunk, force(src, at, plain_chunk))
-            put(dst, i)
-            return carry
-
-        lax.fori_loop(0, plain_count, step, 0)
-
-    last = (xb, xa)[(SUBSTEPS - 1) % 2]
-
-    def drain(src):
-        def step(i, carry):
-            for copy in outputs(src, i):
+            for copy in outputs(src, vel, i):
                 copy.wait()
             return carry
 
         lax.fori_loop(0, plain_count, step, 0)
 
-    pl.when(g == 0)(lambda: drain(xb))
-    pl.when(fine_group)(lambda: drain(last))
-
-    @pl.when(has_high)
-    def _():
-        for k in range(4):
-            halo_copy(k, True).wait_send()
-
-    @pl.when(has_low)
-    def _():
-        for k in range(4):
-            halo_copy(k, False).wait_send()
-
-    for j in range(3):
-        guarded(exists[j], lambda j=j: trace_copy(j).wait_send())
-    pl.when(fine_group & has_high)(lambda: far_copy(True).wait_send())
-    pl.when(fine_group & has_low)(lambda: far_copy(False).wait_send())
-    pltpu.make_async_copy(arrived, arrived, peak_send).wait()
+    @pl.when(g == 0)
+    def _():
+        for i in range(plain_count):
+            put(xb, vel, i)
+        drain(xb, vel)
+
+    @pl.when(g == 1)
+    def _():
+        load = pltpu.make_async_copy(band_hbm, band, load_sem)
+        load.start()
+        size = size_ref[0:1, 0:1]
+        zero = jnp.zeros((HALO, xa.shape[1]), jnp.float32)
+        for buf in (xa, xc):
+            buf[pl.ds(0, HALO), :] = zero
+            buf[pl.ds(total - HALO, HALO), :] = zero
+        load.wait()
+        src, dst, speed = xb, xa, vel
+        for _ in range(SUBSTEPS - 2):
+
+            def step(i, carry, src=src, dst=dst, speed=speed):
+                at = pl.multiple_of(HALO + i * wide_chunk, 8)
+                inner = force(src, band, thick, at, wide_chunk)
+                advance(size, src, dst, speed, held, ext, mass, at, wide_chunk, inner)
+                return carry
+
+            lax.fori_loop(0, wide_count, step, 0)
+            src, dst, speed = dst, (xc if dst is xa else xa), held
+
+        def last_step(i, carry):
+            at = pl.multiple_of(BASE + i * plain_chunk, 8)
+            inner = force(src, band, thick, at, plain_chunk)
+            advance(size, src, dst, speed, held, ext, mass, at, plain_chunk, inner)
+            put(dst, held, i)
+            return carry
+
+        lax.fori_loop(0, plain_count, last_step, 0)
+        drain(dst, held)
 
 
 def per_device(
@@ -462,6 +475,8 @@
     slots = pair_points.shape[3]
     total = rows + 2 * BASE
     blocks = rows // LANES
+    points = pair_points.reshape(3, 1, slots)
+    weights = pair_weights.reshape(3, 1, slots)
     bands = stiff_bands.reshape(stiff_bands.shape[0] * width, width)
     anywhere = pl.BlockSpec(memory_space=pl.ANY)
     vmem = pl.BlockSpec(memory_space=pltpu.VMEM)
@@ -469,19 +484,16 @@
     slim = pltpu.VMEM((total, POINTS), jnp.float32)
     dma = pltpu.SemaphoreType.DMA
     plain_count = rows // row_chunk(rows, 256)
-    return pl.pallas_call(
+    wide_out = pltpu.VMEM((total, width), jnp.float32)
+    slim_out = pltpu.VMEM((total, POINTS), jnp.float32)
+    state = pl.pallas_call(
         functools.partial(kernel, n_grp, n_patch),
-        out_shape=[jax.ShapeDtypeStruct(displace.shape, jnp.float32)] * 2,
-        in_specs=[anywhere] * 6 + [vmem] * 2,
-        out_specs=[anywhere] * 2,
+        out_shape=[wide_out] * 3 + [slim_out] * 2 + [pltpu.VMEM((8, LANES), jnp.float32)],
+        in_specs=[pl.BlockSpec(memory_space=pltpu.HBM)] * 6 + [vmem] * 2,
+        out_specs=[vmem] * 6,
         scratch_shapes=[
             wide,
             wide,
-            wide,
-            wide,
-            wide,
-            slim,
-            slim,
             pltpu.VMEM(bands.shape, jnp.bfloat16),
             pltpu.VMEM((blocks * 16, LANES), jnp.bfloat16),
             pltpu.VMEM((3, 8, slots), jnp.float32),
@@ -497,13 +509,28 @@
             dma((2,)),
             dma,
             dma,
+        ],
+        compiler_params=pltpu.CompilerParams(
+            has_side_effects=True, vmem_limit_bytes=50 * 1024 * 1024
+        ),
+        name="couple_step",
+    )(displace, velocity, ext_force, inv_mass, thickness, bands, points, weights)
+    return pl.pallas_call(
+        steps_kernel,
+        out_shape=[jax.ShapeDtypeStruct(displace.shape, jnp.float32)] * 2,
+        in_specs=[vmem] * 6 + [anywhere],
+        out_specs=[anywhere] * 2,
+        scratch_shapes=[
+            wide,
+            wide,
+            wide,
+            pltpu.VMEM(bands.shape, jnp.bfloat16),
+            dma,
             dma((2, plain_count)),
         ],
-        compiler_params=pltpu.CompilerParams(
-            has_side_effects=True, vmem_limit_bytes=56 * 1024 * 1024
-        ),
-        name="shell_step",
-    )(displace, velocity, ext_force, inv_mass, thickness, bands, pair_points, pair_weights)
+        compiler_params=pltpu.CompilerParams(vmem_limit_bytes=24 * 1024 * 1024),
+        name="fine_steps",
+    )(*state, bands)
 
 
 def solution(mesh):

time: 61.1 us -> 53 us (0.87)
  local copies, waits for them, and re-layouts: 8.25 us -> 0.01 us
    unnamed x6 -> x2, local copies, waits for them, and re-layouts: 8.25 us -> 0.01 us
    pallas_call x1 -> x2, Pallas kernels: 51.9 us -> 52.1 us  [the longest x1 32.5 us: per_device(): pl.pallas_call(functools.partial(kernel, n_grp, n_patch), out_shape=[wide...]
where the time goes in v2:
time: 53 us; the launch traced here: 52.8 us
  Pallas kernels  52.1 us (98%)
  between operations  0.66 us (1%)
    pallas_call x1, Pallas kernels, per_device(): pl.pallas_call(functools.partial(kernel, n_grp, n_patch), out_shape=[wide...  32.5 us
    pallas_call x1, Pallas kernels, per_device(): pl.pallas_call(steps_kernel, out_shape=[jax.ShapeDtypeStruct(displace.sha...  19.6 us

profile of v2, /device:TPU:15, one launch (start us, length us, event | category | flops | bytes accessed | tf_op | source)
XLA Modules:
  0.0 52.8 jit_solution(14259951833360658662)
XLA Ops:
  0.6 0.0 copy-start
  0.6 32.5 %couple_step.1 = (f32[2080,384]{1,0:T(8,128)S(1)}, f32[2080,384]{1,0:T(8,128)S(1)}, f32[2080,384]{1,0:T(8,128)S(1)}, f32[2080,128]{1,0:T(8,128)S(1)}, f32[2080,128]{1,0:T(8,128)S(1)}, /*index=5*/f32[8,128]{1,0:T(8,128)S(1)}) custom-call(f32[1,2048,384]{2,1,0:T(8,128)} %disp_hbm.1, f32[1,2048,384]{2,1,0:T(8,128)} %vel_hbm.1, f32[1,2048,384]{2,1,0:T(8,128)} %ext_hbm.1, ...), custom_call_target="tpu_custom_call" | custom-call | tf_op jit(solution)/shard_map/couple_step/pallas_call | solution.py:489
  33.2 0.0 copy-done
  33.2 19.6 %fine_steps.1 = (f32[1,2048,384]{2,1,0:T(8,128)}, f32[1,2048,384]{2,1,0:T(8,128)}) custom-call(f32[2080,384]{1,0:T(8,128)S(1)} %get-tuple-element.8.xb, f32[2080,384]{1,0:T(8,128)S(1)} %get-tuple-element.9.vel, f32[2080,384]{1,0:T(8,128)S(1)} %get-tuple-element.10.ext, f32[2080,128]{1,0:T(8,128)S(1)} %get-tuple-element.11.mass, ...), custom_call_target="tpu_custom_call" | custom-call | tf_op jit(solution)/shard_map/fine_steps/pallas_call | solution.py:518
Async XLA Ops:
  0.6 32.6 %copy-start = (bf16[5,384,384]{2,1,0:T(8,128)(2,1)S(1)}, bf16[5,384,384]{2,1,0:T(8,128)(2,1)}, u32[]{:S(2)}) copy-start(bf16[5,384,384]{2,1,0:T(8,128)(2,1)} %param.13) | copy-start | bytes 4423684
